TPU v7x, 32 devices: a whole 2x2x4 slice. The times are simulated.
32 devices in a mesh: replica: 8 (over y, x, core), shard: 4 (over z).
Axes of the slice: x: 2, y: 2, z: 4, core: 2. Of those that a mesh axis runs over, the one named last changes fastest.
Arguments:
- inputs: float32 [64, 512, 1024], P(('replica', 'shard')), may hold values from -6 to 6
- lengths: int32 [64], P(('replica', 'shard')), may hold values from 1 to 512, 24576 in all
- cotangent: float32 [64, 512, 1024], P(('replica', 'shard')), may hold values from -6 to 6
- w_in: bfloat16 [2, 1024, 4384], P(None, 'shard'), may hold values from -0.1875 to 0.1875
- w_out: bfloat16 [2, 2048, 1024], P(None, 'shard'), may hold values from -0.125 to 0.125
- norm_gain: float32 [2, 1024], replicated, may hold values from 0.5 to 1.5
- conv_weight: float32 [2, 4, 2304], replicated, may hold values from -3 to 3
- conv_bias: float32 [2, 2304], replicated, may hold values from -3 to 3
- gate_gain: float32 [2, 2048], replicated, may hold values from 0.5 to 1.5
- dt_bias: float32 [2, 32], replicated, may hold values from -6.9 to -2.3
- a_log: float32 [2, 32], replicated, may hold values from 0 to 2.77
- skip: float32 [2, 32], replicated, may hold values from 0.5 to 1.5
Outputs:
- output: float32 [64, 512, 1024], P(('replica', 'shard'))
- input_grad: float32 [64, 512, 1024], P(('replica', 'shard'))
- grad_w_in: float32 [2, 1024, 4384], P(None, 'shard')
- grad_w_out: float32 [2, 2048, 1024], P(None, 'shard')
- grad_norm_gain: float32 [2, 1024], replicated
- grad_conv_weight: float32 [2, 4, 2304], replicated
- grad_conv_bias: float32 [2, 2304], replicated
- grad_gate_gain: float32 [2, 2048], replicated
- grad_dt_bias: float32 [2, 32], replicated
- grad_a_log: float32 [2, 32], replicated
- grad_skip: float32 [2, 32], replicated
Inputs may be any that keep to these rules, and one draw needn't show every extreme that they name: `lengths`: every sequence has at least one token; the longest in each draw has exactly 512.
All inputs are finite; a program needn't handle non-finite values. No bound on the sum of `lengths` on one device may be relied on, other than what follows from the above.
Results may differ from a plain program's by a relative error of at most 0.028.
Values may be sent and summed in bfloat16 or wider, within the bound.
No kernel may reach another device: no remote copies, remote signals or barrier semaphores. Data moves between devices by JAX's collectives and lax.ppermute only.
A program may use at most 320 MiB of HBM per device.

v0:
```python
import jax
import jax.numpy as jnp
from jax import lax
from jax.sharding import PartitionSpec as P

DI = 2048
HEADS = 32
HEAD_DIM = 64
STATE = 128
CONV = 4
SPAN = 256
LEN = 512
EPSILON = 1e-05
HIGHEST = lax.Precision.HIGHEST


def rms_scale(values, gain):
    return values * lax.rsqrt(jnp.mean(values * values, axis=-1, keepdims=True) + EPSILON) * gain


def span_scan(inner_x, step_size, rate, b_input, c_output):
    seq_len = inner_x.shape[0]
    blocks = seq_len // SPAN
    logs = (step_size * rate[None, :]).reshape(blocks, SPAN, HEADS)
    cum_logs = jnp.cumsum(logs, axis=1)
    scaled_x = (inner_x * step_size[:, :, None]).reshape(blocks, SPAN, HEADS, HEAD_DIM)
    b_blocks = b_input.reshape(blocks, SPAN, STATE)
    c_blocks = c_output.reshape(blocks, SPAN, STATE)
    scores = jnp.einsum("cqn,ckn->cqk", c_blocks, b_blocks, precision=HIGHEST)
    row_index = lax.broadcasted_iota(jnp.int32, (SPAN, SPAN), 0)
    col_index = lax.broadcasted_iota(jnp.int32, (SPAN, SPAN), 1)
    causal = (row_index >= col_index)[None, None, :, :]
    cum_heads = jnp.transpose(cum_logs, (0, 2, 1))
    log_gaps = cum_heads[:, :, :, None] - cum_heads[:, :, None, :]
    decays = jnp.where(causal, jnp.exp(jnp.where(causal, log_gaps, 0.0)), 0.0)
    mixing = decays * scores[:, None, :, :]
    intra = jnp.einsum("chqk,ckhp->cqhp", mixing, scaled_x, precision=HIGHEST)
    to_end = jnp.exp(cum_logs[:, -1:, :] - cum_logs)
    states = jnp.einsum(
        "ckhp,ckn->chpn", scaled_x * to_end[:, :, :, None], b_blocks, precision=HIGHEST
    )
    totals = jnp.exp(cum_logs[:, -1, :])
    carried = jnp.zeros((HEADS, HEAD_DIM, STATE), jnp.float32)
    previous = []
    for block in range(blocks):
        previous.append(carried)
        carried = totals[block][:, None, None] * carried + states[block]
    previous = jnp.stack(previous)
    inter = (
        jnp.einsum("cqn,chpn->cqhp", c_blocks, previous, precision=HIGHEST)
        * jnp.exp(cum_logs)[:, :, :, None]
    )
    return (intra + inter).reshape(seq_len, HEADS, HEAD_DIM)


def mix_one(projected, conv_weight, conv_bias, gate_gain, dt_bias, a_log, skip):
    seq_len = projected.shape[0]
    gate_part = projected[:, :DI]
    conv_in = projected[:, DI : 2 * DI + 2 * STATE]
    raw_step = projected[:, 2 * DI + 2 * STATE :]
    padded = jnp.pad(conv_in, ((CONV - 1, 0), (0, 0)))
    pre_act = conv_bias[None, :] + conv_weight[0][None, :] * padded[0:seq_len]
    for offset in range(1, CONV):
        pre_act = pre_act + conv_weight[offset][None, :] * padded[offset : offset + seq_len]
    act = jax.nn.silu(pre_act)
    inner_x = act[:, :DI].reshape(seq_len, HEADS, HEAD_DIM)
    b_input = act[:, DI : DI + STATE]
    c_output = act[:, DI + STATE :]
    step_size = jax.nn.softplus(raw_step + dt_bias[None, :])
    scanned = span_scan(inner_x, step_size, -jnp.exp(a_log), b_input, c_output)
    scanned = scanned + skip[None, :, None] * inner_x
    gated = scanned.reshape(seq_len, DI) * jax.nn.silu(gate_part)
    return rms_scale(gated, gate_gain)


def mix_part(projected, extras):
    by_seq = projected.reshape(-1, LEN, projected.shape[1])
    one_seq = jax.checkpoint(lambda row: mix_one(row, *extras))
    return lax.map(one_seq, by_seq).reshape(projected.shape[0], DI)


def contract_rows(left, right):
    return lax.dot_general(
        left, right, (((0,), (0,)), ((), ())), preferred_element_type=jnp.float32
    )


def contract_cols(left, right):
    return lax.dot_general(
        left, right, (((1,), (1,)), ((), ())), preferred_element_type=jnp.float32
    )


def per_device(
    inputs,
    lengths,
    cotangent,
    w_in,
    w_out,
    norm_gain,
    conv_weight,
    conv_bias,
    gate_gain,
    dt_bias,
    a_log,
    skip,
):
    slot_count, seq_len, width = inputs.shape
    row_total = slot_count * seq_len
    places = lax.broadcasted_iota(jnp.int32, (slot_count, seq_len), 1)
    valid_mask = (places < lengths[:, None]).astype(jnp.float32).reshape(row_total, 1)
    layer_count = w_in.shape[0]
    hidden = inputs.reshape(row_total, width)
    saved = []
    for layer in range(layer_count):
        full_in, full_out = (
            lax.all_gather(w_in[layer], "shard", axis=0, tiled=True),
            lax.all_gather(w_out[layer], "shard", axis=0, tiled=True),
        )
        extras = (
            conv_weight[layer],
            conv_bias[layer],
            gate_gain[layer],
            dt_bias[layer],
            a_log[layer],
            skip[layer],
        )
        normed_full, norm_pull = jax.vjp(rms_scale, hidden, norm_gain[layer])
        normed = normed_full.astype(jnp.bfloat16)
        projected = jnp.dot(normed, full_in, preferred_element_type=jnp.float32)
        mixed_full, mix_pull = jax.vjp(mix_part, projected, extras)
        mixed = mixed_full.astype(jnp.bfloat16)
        branch = jnp.dot(mixed, full_out, preferred_element_type=jnp.float32)
        hidden = hidden + valid_mask * branch
        saved.append((normed, mixed, norm_pull, mix_pull, None, None))
    grad_stream = cotangent.reshape(row_total, width)
    in_parts = [None] * layer_count
    out_parts = [None] * layer_count
    gain_parts = [None] * layer_count
    extra_parts = [None] * layer_count
    for layer in reversed(range(layer_count)):
        normed, mixed, norm_pull, mix_pull, full_in, full_out = saved[layer]
        full_in, full_out = (
            lax.all_gather(w_in[layer], "shard", axis=0, tiled=True),
            lax.all_gather(w_out[layer], "shard", axis=0, tiled=True),
        )
        d_branch = (valid_mask * grad_stream).astype(jnp.bfloat16)
        local_out = contract_rows(mixed, d_branch)
        d_mixed = contract_cols(d_branch, full_out)
        d_projected, d_extras = mix_pull(d_mixed)
        d_proj_low = d_projected.astype(jnp.bfloat16)
        local_in = contract_rows(normed, d_proj_low)
        d_normed = contract_cols(d_proj_low, full_in)
        d_hidden, d_gain = norm_pull(d_normed)
        grad_stream = grad_stream + d_hidden
        owned_in, owned_out = (
            lax.psum_scatter(
                local_in.astype(jnp.bfloat16), "shard", scatter_dimension=0, tiled=True
            ).astype(jnp.float32),
            lax.psum_scatter(
                local_out.astype(jnp.bfloat16), "shard", scatter_dimension=0, tiled=True
            ).astype(jnp.float32),
        )
        owned_in, owned_out = (
            lax.psum(owned_in.astype(jnp.bfloat16), "replica").astype(jnp.float32),
            lax.psum(owned_out.astype(jnp.bfloat16), "replica").astype(jnp.float32),
        )
        in_parts[layer] = owned_in
        out_parts[layer] = owned_out
        gain_parts[layer] = d_gain
        extra_parts[layer] = d_extras
    small_local = (
        jnp.stack(gain_parts),
        jnp.stack([item[0] for item in extra_parts]),
        jnp.stack([item[1] for item in extra_parts]),
        jnp.stack([item[2] for item in extra_parts]),
        jnp.stack([item[3] for item in extra_parts]),
        jnp.stack([item[4] for item in extra_parts]),
        jnp.stack([item[5] for item in extra_parts]),
    )
    summed = lax.psum(
        (
            small_local[0],
            small_local[1],
            small_local[2],
            small_local[3],
            small_local[4],
            small_local[5],
            small_local[6],
        ),
        ("replica", "shard"),
    )
    return (
        hidden.reshape(slot_count, seq_len, width),
        grad_stream.reshape(slot_count, seq_len, width),
        jnp.stack(in_parts),
        jnp.stack(out_parts),
        summed[0],
        summed[1],
        summed[2],
        summed[3],
        summed[4],
        summed[5],
        summed[6],
    )


def solution(mesh):
    in_specs = (
        P(("replica", "shard"), None, None),
        P(("replica", "shard")),
        P(("replica", "shard"), None, None),
        P(None, "shard", None),
        P(None, "shard", None),
        P(),
        P(),
        P(),
        P(),
        P(),
        P(),
        P(),
    )
    out_specs = (
        P(("replica", "shard"), None, None),
        P(("replica", "shard"), None, None),
        P(None, "shard", None),
        P(None, "shard", None),
        P(),
        P(),
        P(),
        P(),
        P(),
        P(),
        P(),
    )
    return jax.shard_map(
        per_device, mesh=mesh, in_specs=in_specs, out_specs=out_specs, check_vma=False
    )
```

profile of v0, /device:TPU:8, one launch (start us, length us, event | category | flops | bytes accessed | tf_op | source)
XLA Modules:
  0.0 2129.3 jit_solution(17221925567403622853)
XLA Ops:
  25.7 64.1 %all-gather.15.cloned.1.call-done = bf16[1,2048,1024]{2,1,0:T(8,128)(2,1)} async-done(((bf16[1,512,1024]{2,1,0:T(8,128)(2,1)}), bf16[1,2048,1024]{2,1,0:T(8,128)(2,1)}) %all-gather.15.cloned.1.call-update) | async-done | bytes 4194320 | tf_op jit(solution)/shard_map/all_gather | solution.py:118
  101.5 147.4 %all-gather.9.cloned.1.call-done = bf16[1,1024,4384]{1,2,0:T(8,128)(2,1)} async-done(((bf16[1,256,4384]{1,2,0:T(8,128)(2,1)}), bf16[1,1024,4384]{1,2,0:T(8,128)(2,1)}) %all-gather.9.cloned.1.call-update) | async-done | bytes 8978448 | tf_op jit(solution)/shard_map/all_gather | solution.py:117
  248.9 17.7 fusion.228
  269.1 195.3 %while.84 = (s32[]{:T(128)}, bf16[2,512,2048]{2,1,0:T(8,128)(2,1)}, f32[1,2304]{1,0:T(1,128)S(1)}, f32[1,2304]{1,0:T(1,128)S(1)}, f32[2,512,4384]{1,2,0:T(8,128)...) while((s32[]{:T(128)}, bf16[2,512,2048]{2,1,0:T(8,128)(2,1)}, ...), condition=%wide.region_5.6_spmd.clone.clone, body=%wide.region_1.5_spmd.clone.clone.sunk | while | flops 5888705024 | bytes 198113264 | solution.py:79
  325.1 20.4 fusion.414
  422.6 20.4 fusion.414
  488.2 13.7 fusion.226
  512.7 439.3 %while.86 = (s32[]{:T(128)}, f32[2304]{0:T(1024)}, f32[4,2304]{1,0:T(4,128)}, f32[32]{0:T(128)}, f32[32]{0:T(128)}, /*index=5*/f32[32]{0:T(128)}, f32[2048]{0:T(...) while((s32[]{:T(128)}, f32[2304]{0:T(1024)}, ...), condition=%wide.region_37.39_spmd.clone, body=%wide.region_12.38_spmd.clone.sunk | while | flops 18517338112 | bytes 734076864 | solution.py:79
  557.1 19.7 bitcast_add_fusion.17
  613.6 26.5 %fusion.456 = (f32[2,32,256]{2,1,0:T(8,128)S(1)}, f32[2,32,256]{2,1,0:T(8,128)}, f32[2,256,256]{2,1,0:T(8,128)S(1)}) fusion(f32[2,256,256]{2,1,0:T(8,128)S(1)} %fusion.452, f32[2,32,256]{2,1,0:T(8,128)S(1)} %get-tuple-element.2367, pred[256,256]{1,0:T(8,128)(4,1)S(1)} %iota_compare_fusion.5, f32[2,256,32,64]{1,0,3,2:T(2,128)} %reshape.1287, ...), kind=kOutput, calls=%fused_computation.112.clone.1 | convolution fusion | flops 3268247552 | bytes 9764864 | tf_op jit(solution)/shard_map/transpose(jvp())/while/body/eval_jaxpr/checkpoint/chqk,ckhp->cqhp/dot_general | solution.py:37
  660.0 15.0 bitcast_add_fusion.18
  773.9 19.7 bitcast_add_fusion.17
  830.4 26.5 %fusion.456 = (f32[2,32,256]{2,1,0:T(8,128)S(1)}, f32[2,32,256]{2,1,0:T(8,128)}, f32[2,256,256]{2,1,0:T(8,128)S(1)}) fusion(f32[2,256,256]{2,1,0:T(8,128)S(1)} %fusion.452, f32[2,32,256]{2,1,0:T(8,128)S(1)} %get-tuple-element.2367, pred[256,256]{1,0:T(8,128)(4,1)S(1)} %iota_compare_fusion.5, f32[2,256,32,64]{1,0,3,2:T(2,128)} %reshape.1287, ...), kind=kOutput, calls=%fused_computation.112.clone.1 | convolution fusion | flops 3268247552 | bytes 9764864 | tf_op jit(solution)/shard_map/transpose(jvp())/while/body/eval_jaxpr/checkpoint/chqk,ckhp->cqhp/dot_general | solution.py:37
  876.8 15.0 bitcast_add_fusion.18
  963.9 16.9 multiply_reduce_fusion.32
  993.6 211.0 %while.85 = (s32[]{:T(128)}, bf16[2,512,2048]{2,1,0:T(8,128)(2,1)}, f32[1,2304]{1,0:T(1,128)S(1)}, f32[1,2304]{1,0:T(1,128)S(1)}, f32[2,512,4384]{1,2,0:T(8,128)...) while((s32[]{:T(128)}, bf16[2,512,2048]{2,1,0:T(8,128)(2,1)}, ...), condition=%wide.region_11.12_spmd.clone.clone, body=%wide.region_7.11_spmd.clone.clone.sunk | while | flops 5888705024 | bytes 198113264 | solution.py:79
  1065.4 20.4 fusion.427
  1162.5 20.4 fusion.427
  1215.4 16.5 convolution_convert_fusion
  1248.2 460.2 %while.87 = (s32[]{:T(128)}, f32[2304]{0:T(1024)}, f32[4,2304]{1,0:T(4,128)}, f32[32]{0:T(128)}, f32[32]{0:T(128)}, /*index=5*/f32[32]{0:T(128)}, f32[2048]{0:T(...) while((s32[]{:T(128)}, f32[2304]{0:T(1024)}, ...), condition=%wide.region_64.66_spmd.clone, body=%wide.region_39.65_spmd.clone.sunk | while | flops 18517338112 | bytes 706551744 | solution.py:79
  1302.3 19.7 bitcast_add_fusion.19
  1359.2 26.5 %fusion.488 = (f32[2,32,256]{2,1,0:T(8,128)S(1)}, f32[2,32,256]{2,1,0:T(8,128)}, f32[2,256,256]{2,1,0:T(8,128)S(1)}) fusion(f32[2,256,256]{2,1,0:T(8,128)S(1)} %fusion.484, f32[2,32,256]{2,1,0:T(8,128)S(1)} %get-tuple-element.2434, pred[256,256]{1,0:T(8,128)(4,1)S(1)} %iota_compare_fusion.6, f32[2,256,32,64]{1,0,3,2:T(2,128)} %reshape.1293, ...), kind=kOutput, calls=%fused_computation.257.clone.1 | convolution fusion | flops 3268247552 | bytes 9764864 | tf_op jit(solution)/shard_map/transpose(jvp())/while/body/eval_jaxpr/checkpoint/chqk,ckhp->cqhp/dot_general | solution.py:37
  1405.7 15.0 bitcast_add_fusion.20
  1528.9 19.7 bitcast_add_fusion.19
  1585.6 26.5 %fusion.488 = (f32[2,32,256]{2,1,0:T(8,128)S(1)}, f32[2,32,256]{2,1,0:T(8,128)}, f32[2,256,256]{2,1,0:T(8,128)S(1)}) fusion(f32[2,256,256]{2,1,0:T(8,128)S(1)} %fusion.484, f32[2,32,256]{2,1,0:T(8,128)S(1)} %get-tuple-element.2434, pred[256,256]{1,0:T(8,128)(4,1)S(1)} %iota_compare_fusion.6, f32[2,256,32,64]{1,0,3,2:T(2,128)} %reshape.1293, ...), kind=kOutput, calls=%fused_computation.257.clone.1 | convolution fusion | flops 3268247552 | bytes 9764864 | tf_op jit(solution)/shard_map/transpose(jvp())/while/body/eval_jaxpr/checkpoint/chqk,ckhp->cqhp/dot_general | solution.py:37
  1632.0 15.0 bitcast_add_fusion.20
  1708.4 15.8 bitcast_convert_fusion
  1724.3 155.1 %reduce-scatter.5.cloned.1.call-done = bf16[256,4384]{0,1:T(8,128)(2,1)} async-done(((bf16[1024,4384]{0,1:T(8,128)(2,1)}), bf16[256,4384]{0,1:T(8,128)(2,1)}) %reduce-scatter.5.cloned.1.call-update) | async-done | bytes 2244624 | tf_op jit(solution)/shard_map/reduce_scatter | solution.py:157
  1891.6 17.5 fusion.244
  1917.5 42.3 %all-reduce.44 = (f32[2,1024]{1,0:T(2,128)}, f32[2,2304]{1,0:T(2,128)}, f32[2,2048]{1,0:T(2,128)}, f32[2,32]{1,0:T(2,128)}, f32[2,32]{1,0:T(2,128)}, /*index=5*/f32[2,32]{1,0:T(2,128)}) all-reduce(f32[2,1024]{1,0:T(2,128)S(1)} %pad_maximum_fusion.3, ...), channel_id=1, replica_groups=mesh['replica'=8,'shard'=4] {'replica','shard'}, use_global_device_ids=true, to_apply=%region_76.78 | all-reduce | flops 10944 | bytes 87552 | tf_op jit(solution)/shard_map/psum | solution.py:181
  1971.8 21.3 %all-reduce.51.cloned.1.call-done = (bf16[1,256,4384]{1,2,0:T(8,128)(2,1)}, bf16[1,256,4384]{1,2,0:T(8,128)(2,1)}, bf16[1,512,1024]{2,1,0:T(8,128)(2,1)}, bf16[1,512,1024]{2,1,0:T(8,128)(2,1)}) async-done(((bf16[1,256,4384]{1,2,0:T(8,128)(2,1)}, bf16[1,256,4384]{1,2,0:T(8,128)(2,1)}, bf16[1,512,1024]{2,1,0:T(8,128)(2,1)}, bf16[1,512,1024]{2,1,0:T(8,128)(2,1)}), (bf16[1,256,4384]{1,2,0:T(8,128)(2,1)}, ...) | async-done | bytes 6586384 | tf_op jit(solution)/shard_map/psum | solution.py:165
  2002.1 118.3 %all-reduce.49.cloned.1.call-done = f32[2,4,2304]{2,1,0:T(4,128)} async-done(((f32[2,4,2304]{2,1,0:T(4,128)}), f32[2,4,2304]{2,1,0:T(4,128)}) %all-reduce.49.cloned.1.call-update) | async-done | bytes 73744 | tf_op jit(solution)/shard_map/psum | solution.py:181
  (1105 shorter events, 1105.4 us)
Async XLA Ops:
  7.2 82.6 %all-gather.15.cloned.1.call-start = ((), (), s32[]{:S(2)}) async-start(), calls=%async_computation.12 | async-start | bytes 5242880 | tf_op jit(solution)/shard_map/all_gather | solution.py:118
  10.3 238.6 %all-gather.9.cloned.1.call-start = ((), (), s32[]{:S(2)}) async-start(), calls=%async_computation.9 | async-start | bytes 11223040 | tf_op jit(solution)/shard_map/all_gather | solution.py:117
  15.2 449.3 %all-gather.11.cloned.1.call-start = ((), (), s32[]{:S(2)}) async-start(), calls=%async_computation.10 | async-start | bytes 5242880 | tf_op jit(solution)/shard_map/all_gather | solution.py:118
  15.9 472.3 %all-gather.13.cloned.1.call-start = ((), (), s32[]{:S(2)}) async-start(), calls=%async_computation.11 | async-start | bytes 11223040 | tf_op jit(solution)/shard_map/all_gather | solution.py:117
  16.5 1707.7 %reduce-scatter.9.cloned.1.call-start = ((), (), s32[]{:S(2)}) async-start(), calls=%async_computation.6 | async-start | bytes 5242880 | tf_op jit(solution)/shard_map/reduce_scatter | solution.py:160
  18.5 230.4 %copy-start.121 = (f32[1,1024]{1,0:T(1,128)}, f32[1,1024]{1,0:T(1,128)S(1)}, u32[]{:S(2)}) copy-start(f32[1,1024]{1,0:T(1,128)S(1)} %get-tuple-element.1838) | copy-start | bytes 12292
  22.1 226.9 %copy-start.131 = (f32[2,512]{1,0:T(2,128)}, f32[2,512]{1,0:T(2,128)S(1)}, u32[]{:S(2)}) copy-start(f32[2,512]{1,0:T(2,128)S(1)} %get-tuple-element.1840) | copy-start | bytes 12292
  24.5 76.9 %copy-start.136 = (f32[2,512]{1,0:T(2,128)}, f32[2,512]{1,0:T(2,128)S(1)}, u32[]{:S(2)}) copy-start(f32[2,512]{1,0:T(2,128)S(1)} %get-tuple-element.1853) | copy-start | bytes 12292
  269.1 195.4 %copy-start.132 = (f32[1,4,2,128]{3,1,2,0:T(4,128)S(1)}, f32[1,4,2,128]{3,1,2,0:T(4,128)}, u32[]{:S(2)}) copy-start(f32[1,4,2,128]{3,1,2,0:T(4,128)} %copy.386) | copy-start | bytes 12292
  464.5 23.7 %copy-start.123 = (f32[1,1024]{1,0:T(1,128)S(1)}, f32[1,1024]{1,0:T(1,128)}, u32[]{:S(2)}) copy-start(f32[1,1024]{1,0:T(1,128)} %get-tuple-element.1837) | copy-start | bytes 12292
  475.8 26.1 %copy-start.127 = (f32[1024]{0:T(1024)}, f32[1024]{0:T(1024)S(1)}, u32[]{:S(2)}) copy-start(f32[1024]{0:T(1024)S(1)} %get-tuple-element.1855) | copy-start | bytes 12292
  475.8 26.1 %copy-start.118 = (f32[1024]{0:T(1024)}, f32[1024]{0:T(1024)S(1)}, u32[]{:S(2)}) copy-start(f32[1024]{0:T(1024)S(1)} %fusion.249) | copy-start | bytes 12292
  536.8 76.8 %copy-start.40 = (f32[2,32,256]{2,1,0:T(8,128)}, f32[2,32,256]{2,1,0:T(8,128)S(1)}, u32[]{:S(2)}) copy-start(f32[2,32,256]{2,1,0:T(8,128)S(1)} %get-tuple-element.2367) | copy-start | bytes 196612 | tf_op jit(solution)/shard_map/transpose(jvp())/while
  557.1 56.5 %copy-start.44 = (pred[256,256]{1,0:T(8,128)(4,1)}, pred[256,256]{1,0:T(8,128)(4,1)S(1)}, u32[]{:S(2)}) copy-start(pred[256,256]{1,0:T(8,128)(4,1)S(1)} %iota_compare_fusion.5) | copy-start | bytes 196612 | tf_op jit(solution)/shard_map/transpose(jvp())/while
  753.6 76.8 %copy-start.40 = (f32[2,32,256]{2,1,0:T(8,128)}, f32[2,32,256]{2,1,0:T(8,128)S(1)}, u32[]{:S(2)}) copy-start(f32[2,32,256]{2,1,0:T(8,128)S(1)} %get-tuple-element.2367) | copy-start | bytes 196612 | tf_op jit(solution)/shard_map/transpose(jvp())/while
  773.9 56.5 %copy-start.44 = (pred[256,256]{1,0:T(8,128)(4,1)}, pred[256,256]{1,0:T(8,128)(4,1)S(1)}, u32[]{:S(2)}) copy-start(pred[256,256]{1,0:T(8,128)(4,1)S(1)} %iota_compare_fusion.5) | copy-start | bytes 196612 | tf_op jit(solution)/shard_map/transpose(jvp())/while
  991.0 733.3 %reduce-scatter.11.cloned.1.call-start = ((), (), s32[]{:S(2)}) async-start(), calls=%async_computation.7 | async-start | bytes 5242880 | tf_op jit(solution)/shard_map/reduce_scatter | solution.py:160
  993.6 211.0 %copy-start.137 = (f32[2,512]{1,0:T(2,128)S(1)}, f32[2,512]{1,0:T(2,128)}, u32[]{:S(2)}) copy-start(f32[2,512]{1,0:T(2,128)} %copy-done.136) | copy-start | bytes 12292
  1214.7 509.6 %reduce-scatter.7.cloned.1.call-start = ((), (), s32[]{:S(2)}) async-start(), calls=%async_computation.5 | async-start | bytes 11223040 | tf_op jit(solution)/shard_map/reduce_scatter | solution.py:157
  1231.9 647.5 %reduce-scatter.5.cloned.1.call-start = ((), (), s32[]{:S(2)}) async-start(), calls=%async_computation.4 | async-start | bytes 11223040 | tf_op jit(solution)/shard_map/reduce_scatter | solution.py:157
  1282.1 77.1 %copy-start.42 = (f32[2,32,256]{2,1,0:T(8,128)}, f32[2,32,256]{2,1,0:T(8,128)S(1)}, u32[]{:S(2)}) copy-start(f32[2,32,256]{2,1,0:T(8,128)S(1)} %get-tuple-element.2434) | copy-start | bytes 196612 | tf_op jit(solution)/shard_map/transpose(jvp())/while
  1302.3 56.8 %copy-start.46 = (pred[256,256]{1,0:T(8,128)(4,1)}, pred[256,256]{1,0:T(8,128)(4,1)S(1)}, u32[]{:S(2)}) copy-start(pred[256,256]{1,0:T(8,128)(4,1)S(1)} %iota_compare_fusion.6) | copy-start | bytes 196612 | tf_op jit(solution)/shard_map/transpose(jvp())/while
  1508.7 76.8 %copy-start.42 = (f32[2,32,256]{2,1,0:T(8,128)}, f32[2,32,256]{2,1,0:T(8,128)S(1)}, u32[]{:S(2)}) copy-start(f32[2,32,256]{2,1,0:T(8,128)S(1)} %get-tuple-element.2434) | copy-start | bytes 196612 | tf_op jit(solution)/shard_map/transpose(jvp())/while
  1528.9 56.6 %copy-start.46 = (pred[256,256]{1,0:T(8,128)(4,1)}, pred[256,256]{1,0:T(8,128)(4,1)S(1)}, u32[]{:S(2)}) copy-start(pred[256,256]{1,0:T(8,128)(4,1)S(1)} %iota_compare_fusion.6) | copy-start | bytes 196612 | tf_op jit(solution)/shard_map/transpose(jvp())/while
  1724.2 155.3 %copy-start.126 = (f32[1,4,2,128]{3,2,1,0:T(2,128)S(1)}, f32[1,4,2,128]{3,2,1,0:T(2,128)}, u32[]{:S(2)}) copy-start(f32[1,4,2,128]{3,2,1,0:T(2,128)} %get-tuple-element.1839) | copy-start | bytes 12292
  1724.2 269.0 %all-reduce.51.cloned.1.call-start = ((), (), s32[]{:S(2)}) async-start(), calls=%async_computation.13 | async-start | bytes 13172736 | tf_op jit(solution)/shard_map/psum | solution.py:165
  1879.5 240.9 %all-reduce.49.cloned.1.call-start = ((), (), s32[]{:S(2)}) async-start(), calls=%async_computation.8 | async-start | bytes 147456 | tf_op jit(solution)/shard_map/psum | solution.py:181
  1891.6 18.4 copy-start.108
  1891.6 18.4 copy-start.71
  1891.6 18.4 copy-start.74
  1891.6 18.4 copy-start.138
  1910.1 49.8 %copy-start.135 = (f32[1,4,2,128]{3,1,2,0:T(4,128)S(1)}, f32[1,4,2,128]{3,1,2,0:T(4,128)}, u32[]{:S(2)}) copy-start(f32[1,4,2,128]{3,1,2,0:T(4,128)} %copy.386) | copy-start | bytes 12292
  (244 other events, 1279.1 us)
Sparse Core Ops, SparseCore 0:
  10.5 79.2 all-gather.14
  91.9 156.9 all-gather.8
  250.5 79.2 all-gather.10
  331.2 156.9 all-gather.12
  991.1 77.9 reduce-scatter.8
  1214.8 78.0 reduce-scatter.10
  1295.2 154.1 reduce-scatter.6
  1724.3 155.1 reduce-scatter.4
  1883.2 109.8 all-reduce.50
  1999.2 121.1 all-reduce.48
where the time goes:
time: 2140 us; the launch traced here: 2130 us
  matrix products  667 us (31%)
  waiting for transfers between devices  520 us (24%)
  other arithmetic  425 us (20%)
  local copies, waits for them, and re-layouts  424 us (20%)
  blocking collectives  42.3 us (2%)
  loops' own time  34.9 us (2%)
    dot_general x16, matrix products, span_scan(): intra = jnp.einsum('chqk,ckhp->cqhp', mixing, scaled_x, precision=HIGHEST)  327 us
    all_gather x2, waiting for transfers between devices, per_device(): lax.all_gather(w_in[layer], 'shard', axis=0, tiled=True)  160 us
    reduce_scatter x2, waiting for transfers between devices, per_device(): lax.psum_scatter(local_in.astype(jnp.bfloat16), 'shard', scatter_dimensio...  155 us
    psum x1, waiting for transfers between devices, per_device(): lax.psum((small_local[0], small_local[1], small_local[2], small_local[3],...  118 us
    mul x8, other arithmetic, mix_one(): act = jax.nn.silu(pre_act)  83.6 us
    while x416, local copies, waits for them, and re-layouts  80.3 us
    mul x20, other arithmetic, mix_one(): conv_weight[offset][None, :] * padded[offset:offset + seq_len]  67.5 us
    dot_general x12, matrix products, span_scan(): jnp.einsum('cqn,chpn->cqhp', c_blocks, previous, precision=HIGHEST)  64.9 us
  transfers between devices with their start and end apart: 10, of which 6 were waited for; matrix products, arithmetic and copies ran while one was open for 46% of the time, Pallas kernels for 0%

commit v1 on v0

--- a/solution.py
+++ b/solution.py
@@ -12,6 +12,27 @@
 LEN = 512
 EPSILON = 1e-05
 HIGHEST = lax.Precision.HIGHEST
+
+
+def collect(x, axis, dim):
+    devices, place, rows = (lax.axis_size(axis), lax.axis_index(axis), x.shape[dim])
+    forward = [(i, (i + 1) % devices) for i in range(devices)]
+    left = [(i, (i - 1) % devices) for i in range(devices)]
+    out = jnp.zeros((*x.shape[:dim], devices * rows, *x.shape[dim + 1 :]), x.dtype)
+    out = lax.dynamic_update_slice_in_dim(out, x, place * rows, axis=dim)
+    from_left = from_right = x
+    middle = devices // 2
+    for step in range(1, middle + 1):
+        from_left = lax.ppermute(from_left, axis, forward)
+        out = lax.dynamic_update_slice_in_dim(
+            out, from_left, (place - step) % devices * rows, axis=dim
+        )
+        if step < devices - middle:
+            from_right = lax.ppermute(from_right, axis, left)
+            out = lax.dynamic_update_slice_in_dim(
+                out, from_right, (place + step) % devices * rows, axis=dim
+            )
+    return out
 
 
 def rms_scale(values, gain):
@@ -115,7 +136,7 @@
     for layer in range(layer_count):
         full_in, full_out = (
             lax.all_gather(w_in[layer], "shard", axis=0, tiled=True),
-            lax.all_gather(w_out[layer], "shard", axis=0, tiled=True),
+            collect(w_out[layer], "shard", 0),
         )
         extras = (
             conv_weight[layer],

time: 2140 us -> 2250 us (1.051)
  waiting for transfers between devices: 520 us -> 590 us
  starting transfers between devices: 0.57 us -> 27.7 us
    ppermute x0 -> x6, waiting for transfers between devices: none -> 205 us  [the longest x4 205 us: collect(): from_left = lax.ppermute(from_left, axis, forward)]
    all_gather x2, waiting for transfers between devices: 160 us -> 84.4 us  [per_device(): lax.all_gather(w_in[layer], 'shard', axis=0, tiled=True)]
    all_gather x2, waiting for transfers between devices: 64.1 us -> 0.02 us  [per_device(): lax.all_gather(w_out[layer], 'shard', axis=0, tiled=True)]
    ppermute x0 -> x6, starting transfers between devices: none -> 27.1 us  [the longest x4 26.1 us: collect(): from_left = lax.ppermute(from_left, axis, forward)]
  transfers between devices with their start and end apart: 10 -> 16, of which waited for: 6 -> 7; matrix products, arithmetic and copies ran while one was open for 46% -> 65% of each run, Pallas kernels for 0% -> 0%
where the time goes in v1:
time: 2250 us; the launch traced here: 2240 us
  matrix products  664 us (30%)
  waiting for transfers between devices  590 us (26%)
  local copies, waits for them, and re-layouts  442 us (20%)
  other arithmetic  422 us (19%)
  blocking collectives  41.4 us (2%)
  loops' own time  37.3 us (2%)
  starting transfers between devices  27.7 us (1%)
    dot_general x16, matrix products, span_scan(): intra = jnp.einsum('chqk,ckhp->cqhp', mixing, scaled_x, precision=HIGHEST)  327 us
    ppermute x4, waiting for transfers between devices, collect(): from_left = lax.ppermute(from_left, axis, forward)  205 us
    reduce_scatter x2, waiting for transfers between devices, per_device(): lax.psum_scatter(local_in.astype(jnp.bfloat16), 'shard', scatter_dimensio...  157 us
    psum x1, waiting for transfers between devices, per_device(): lax.psum((small_local[0], small_local[1], small_local[2], small_local[3],...  118 us
    all_gather x2, waiting for transfers between devices, per_device(): lax.all_gather(w_in[layer], 'shard', axis=0, tiled=True)  84.4 us
    mul x8, other arithmetic, mix_one(): act = jax.nn.silu(pre_act)  83.6 us
    while x416, local copies, waits for them, and re-layouts  81.1 us
    mul x20, other arithmetic, mix_one(): conv_weight[offset][None, :] * padded[offset:offset + seq_len]  67.2 us
  transfers between devices with their start and end apart: 16, of which 7 were waited for; matrix products, arithmetic and copies ran while one was open for 65% of the time, Pallas kernels for 0%

profile of v1, /device:TPU:8, one launch (start us, length us, event | category | flops | bytes accessed | tf_op | source)
XLA Modules:
  0.0 2239.8 jit_solution(3595817546587712184)
XLA Ops:
  31.6 124.7 %collective-permute-done = bf16[512,1024]{1,0:T(8,128)(2,1)} collective-permute-done((bf16[512,1024]{1,0:T(8,128)(2,1)}, bf16[512,1024]{1,0:T(8,128)(2,1)}, u32[]{:S(2)}, u32[]{:S(2)}) %collective-permute-start) | collective-permute-done | bytes 1048608 | tf_op jit(solution)/shard_map/ppermute | solution.py:26
  156.3 21.0 collective-permute-start.2
  188.5 58.7 %collective-permute-done.2 = bf16[512,1024]{1,0:T(8,128)(2,1)S(1)} collective-permute-done((bf16[512,1024]{1,0:T(8,128)(2,1)}, bf16[512,1024]{1,0:T(8,128)(2,1)S(1)}, u32[]{:S(2)}, u32[]{:S(2)}) %collective-permute-start.2) | collective-permute-done | bytes 1048608 | tf_op jit(solution)/shard_map/ppermute | solution.py:26
  247.2 21.7 collective-permute-done.5
  281.8 84.4 %all-gather.9.cloned.1.call-done = bf16[1,1024,4384]{1,2,0:T(8,128)(2,1)} async-done(((bf16[1,256,4384]{1,2,0:T(8,128)(2,1)}), bf16[1,1024,4384]{1,2,0:T(8,128)(2,1)}) %all-gather.9.cloned.1.call-update) | async-done | bytes 8978448 | tf_op jit(solution)/shard_map/all_gather | solution.py:138
  366.2 17.7 fusion.228
  386.5 196.0 %while.84 = (s32[]{:T(128)}, bf16[2,512,2048]{2,1,0:T(8,128)(2,1)}, f32[1,2304]{1,0:T(1,128)S(1)}, f32[1,2304]{1,0:T(1,128)S(1)}, f32[2,512,4384]{1,2,0:T(8,128)...) while((s32[]{:T(128)}, bf16[2,512,2048]{2,1,0:T(8,128)(2,1)}, ...), condition=%wide.region_5.6_spmd.clone.clone, body=%wide.region_1.5_spmd.clone.clone.sunk | while | flops 5888705024 | bytes 198113264 | solution.py:100
  442.7 20.4 fusion.408
  540.5 20.4 fusion.408
  618.6 439.0 %while.86 = (s32[]{:T(128)}, f32[2304]{0:T(1024)}, f32[4,2304]{1,0:T(4,128)}, f32[32]{0:T(128)}, f32[32]{0:T(128)}, /*index=5*/f32[32]{0:T(128)}, f32[2048]{0:T(...) while((s32[]{:T(128)}, f32[2304]{0:T(1024)}, ...), condition=%wide.region_37.39_spmd.clone, body=%wide.region_12.38_spmd.clone.sunk | while | flops 18517338112 | bytes 734076864 | solution.py:100
  663.0 19.7 bitcast_add_fusion.17
  719.5 26.5 %fusion.450 = (f32[2,32,256]{2,1,0:T(8,128)S(1)}, f32[2,32,256]{2,1,0:T(8,128)}, f32[2,256,256]{2,1,0:T(8,128)S(1)}) fusion(f32[2,256,256]{2,1,0:T(8,128)S(1)} %fusion.446, f32[2,32,256]{2,1,0:T(8,128)S(1)} %get-tuple-element.2371, pred[256,256]{1,0:T(8,128)(4,1)S(1)} %iota_compare_fusion.5, f32[2,256,32,64]{1,0,3,2:T(2,128)} %reshape.1287, ...), kind=kOutput, calls=%fused_computation.112.clone.1 | convolution fusion | flops 3268247552 | bytes 9764864 | tf_op jit(solution)/shard_map/transpose(jvp())/while/body/eval_jaxpr/checkpoint/chqk,ckhp->cqhp/dot_general | solution.py:58
  765.9 15.0 bitcast_add_fusion.18
  879.6 19.7 bitcast_add_fusion.17
  936.2 26.5 %fusion.450 = (f32[2,32,256]{2,1,0:T(8,128)S(1)}, f32[2,32,256]{2,1,0:T(8,128)}, f32[2,256,256]{2,1,0:T(8,128)S(1)}) fusion(f32[2,256,256]{2,1,0:T(8,128)S(1)} %fusion.446, f32[2,32,256]{2,1,0:T(8,128)S(1)} %get-tuple-element.2371, pred[256,256]{1,0:T(8,128)(4,1)S(1)} %iota_compare_fusion.5, f32[2,256,32,64]{1,0,3,2:T(2,128)} %reshape.1287, ...), kind=kOutput, calls=%fused_computation.112.clone.1 | convolution fusion | flops 3268247552 | bytes 9764864 | tf_op jit(solution)/shard_map/transpose(jvp())/while/body/eval_jaxpr/checkpoint/chqk,ckhp->cqhp/dot_general | solution.py:58
  982.5 15.0 bitcast_add_fusion.18
  1069.4 16.9 multiply_reduce_fusion.32
  1099.1 210.9 %while.85 = (s32[]{:T(128)}, bf16[2,512,2048]{2,1,0:T(8,128)(2,1)}, f32[1,2304]{1,0:T(1,128)S(1)}, f32[1,2304]{1,0:T(1,128)S(1)}, f32[2,512,4384]{1,2,0:T(8,128)...) while((s32[]{:T(128)}, bf16[2,512,2048]{2,1,0:T(8,128)(2,1)}, ...), condition=%wide.region_11.12_spmd.clone.clone, body=%wide.region_7.11_spmd.clone.clone.sunk | while | flops 5888705024 | bytes 198113264 | solution.py:100
  1170.8 20.4 fusion.421
  1267.9 20.4 fusion.421
  1320.8 16.5 convolution_convert_fusion
  1353.4 463.8 %while.87 = (s32[]{:T(128)}, f32[2304]{0:T(1024)}, f32[4,2304]{1,0:T(4,128)}, f32[32]{0:T(128)}, f32[32]{0:T(128)}, /*index=5*/f32[32]{0:T(128)}, f32[2048]{0:T(...) while((s32[]{:T(128)}, f32[2304]{0:T(1024)}, ...), condition=%wide.region_64.66_spmd.clone, body=%wide.region_39.0_spmd.clone.sunk | while | flops 18517338112 | bytes 706551744 | solution.py:100
  1407.8 19.7 bitcast_add_fusion.19
  1465.0 26.5 %fusion.482 = (f32[2,32,256]{2,1,0:T(8,128)S(1)}, f32[2,32,256]{2,1,0:T(8,128)}, f32[2,256,256]{2,1,0:T(8,128)S(1)}) fusion(f32[2,256,256]{2,1,0:T(8,128)S(1)} %fusion.478, f32[2,32,256]{2,1,0:T(8,128)S(1)} %get-tuple-element.2438, pred[256,256]{1,0:T(8,128)(4,1)S(1)} %iota_compare_fusion.6, f32[2,256,32,64]{1,0,3,2:T(2,128)} %reshape.1293, ...), kind=kOutput, calls=%fused_computation.257.clone.1 | convolution fusion | flops 3268247552 | bytes 9764864 | tf_op jit(solution)/shard_map/transpose(jvp())/while/body/eval_jaxpr/checkpoint/chqk,ckhp->cqhp/dot_general | solution.py:58
  1634.9 19.7 bitcast_add_fusion.19
  1692.1 26.5 %fusion.482 = (f32[2,32,256]{2,1,0:T(8,128)S(1)}, f32[2,32,256]{2,1,0:T(8,128)}, f32[2,256,256]{2,1,0:T(8,128)S(1)}) fusion(f32[2,256,256]{2,1,0:T(8,128)S(1)} %fusion.478, f32[2,32,256]{2,1,0:T(8,128)S(1)} %get-tuple-element.2438, pred[256,256]{1,0:T(8,128)(4,1)S(1)} %iota_compare_fusion.6, f32[2,256,32,64]{1,0,3,2:T(2,128)} %reshape.1293, ...), kind=kOutput, calls=%fused_computation.257.clone.1 | convolution fusion | flops 3268247552 | bytes 9764864 | tf_op jit(solution)/shard_map/transpose(jvp())/while/body/eval_jaxpr/checkpoint/chqk,ckhp->cqhp/dot_general | solution.py:58
  1817.2 15.7 bitcast_convert_fusion
  1833.1 156.7 %reduce-scatter.5.cloned.1.call-done = bf16[256,4384]{0,1:T(8,128)(2,1)} async-done(((bf16[1024,4384]{0,1:T(8,128)(2,1)}), bf16[256,4384]{0,1:T(8,128)(2,1)}) %reduce-scatter.5.cloned.1.call-update) | async-done | bytes 2244624 | tf_op jit(solution)/shard_map/reduce_scatter | solution.py:178
  2001.9 17.5 fusion.240
  2037.8 41.4 %all-reduce.44 = (f32[2,1024]{1,0:T(2,128)}, f32[2,2304]{1,0:T(2,128)}, f32[2,2048]{1,0:T(2,128)}, f32[2,32]{1,0:T(2,128)}, f32[2,32]{1,0:T(2,128)}, /*index=5*/f32[2,32]{1,0:T(2,128)}) all-reduce(f32[2,1024]{1,0:T(2,128)S(1)} %pad_maximum_fusion.3, ...), channel_id=1, replica_groups=mesh['replica'=8,'shard'=4] {'replica','shard'}, use_global_device_ids=true, to_apply=%region_76.78 | all-reduce | flops 10944 | bytes 87552 | tf_op jit(solution)/shard_map/psum | solution.py:202
  2079.2 24.7 %all-reduce.51.cloned.1.call-done = (bf16[1,256,4384]{1,2,0:T(8,128)(2,1)}, bf16[1,256,4384]{1,2,0:T(8,128)(2,1)}, bf16[1,512,1024]{2,1,0:T(8,128)(2,1)}, bf16[1,512,1024]{2,1,0:T(8,128)(2,1)}) async-done(((bf16[1,256,4384]{1,2,0:T(8,128)(2,1)}, bf16[1,256,4384]{1,2,0:T(8,128)(2,1)}, bf16[1,512,1024]{2,1,0:T(8,128)(2,1)}, bf16[1,512,1024]{2,1,0:T(8,128)(2,1)}), (bf16[1,256,4384]{1,2,0:T(8,128)(2,1)}, ...) | async-done | bytes 6586384 | tf_op jit(solution)/shard_map/psum | solution.py:186
  2112.9 118.3 %all-reduce.49.cloned.1.call-done = f32[2,4,2304]{2,1,0:T(4,128)} async-done(((f32[2,4,2304]{2,1,0:T(4,128)}), f32[2,4,2304]{2,1,0:T(4,128)}) %all-reduce.49.cloned.1.call-update) | async-done | bytes 73744 | tf_op jit(solution)/shard_map/psum | solution.py:202
  (1136 shorter events, 1154.6 us)
Async XLA Ops:
  7.2 263.2 %all-gather.13.cloned.1.call-start = ((), (), s32[]{:S(2)}) async-start(), calls=%async_computation.11 | async-start | bytes 5242880 | tf_op jit(solution)/shard_map/all_gather | solution.py:166
  11.1 355.1 %all-gather.9.cloned.1.call-start = ((), (), s32[]{:S(2)}) async-start(), calls=%async_computation.9 | async-start | bytes 11223040 | tf_op jit(solution)/shard_map/all_gather | solution.py:138
  15.9 578.1 %all-gather.11.cloned.1.call-start = ((), (), s32[]{:S(2)}) async-start(), calls=%async_computation.10 | async-start | bytes 11223040 | tf_op jit(solution)/shard_map/all_gather | solution.py:138
  16.6 1320.9 %all-gather.15.cloned.1.call-start = ((), (), s32[]{:S(2)}) async-start(), calls=%async_computation.12 | async-start | bytes 5242880 | tf_op jit(solution)/shard_map/all_gather | solution.py:166
  16.7 160.6 %collective-permute-start.3 = (bf16[512,1024]{1,0:T(8,128)(2,1)}, bf16[512,1024]{1,0:T(8,128)(2,1)S(1)}, u32[]{:S(2)}, u32[]{:S(2)}) collective-permute-start(bf16[512,1024]{1,0:T(8,128)(2,1)} %get-tuple-element.1823), channel_id=1, source_target_pairs={{0,1},{1,2},{2,3},{3,0},{4,5},{5,6},{6,7},{7,4},{8,9},{9,10},{10,1... | collective-permute-start | bytes 3145736 | tf_op jit(solution)/shard_map/ppermute | solution.py:26
  18.3 165.6 %collective-permute-start.4 = (bf16[512,1024]{1,0:T(8,128)(2,1)}, bf16[512,1024]{1,0:T(8,128)(2,1)}, u32[]{:S(2)}, u32[]{:S(2)}) collective-permute-start(bf16[512,1024]{1,0:T(8,128)(2,1)} %get-tuple-element.1823), channel_id=1, source_target_pairs={{0,3},{1,0},{2,1},{3,2},{4,7},{5,4},{6,5},{7,6},{8,11},{9,8},{10,9... | collective-permute-start | bytes 3145736 | tf_op jit(solution)/shard_map/ppermute | solution.py:31
  18.7 137.6 %collective-permute-start = (bf16[512,1024]{1,0:T(8,128)(2,1)}, bf16[512,1024]{1,0:T(8,128)(2,1)}, u32[]{:S(2)}, u32[]{:S(2)}) collective-permute-start(bf16[512,1024]{1,0:T(8,128)(2,1)} %get-tuple-element.1822), channel_id=1, source_target_pairs={{0,1},{1,2},{2,3},{3,0},{4,5},{5,6},{6,7},{7,4},{8,9},{9,10},{10,1... | collective-permute-start | bytes 3145736 | tf_op jit(solution)/shard_map/ppermute | solution.py:26
  20.3 165.9 %collective-permute-start.1 = (bf16[512,1024]{1,0:T(8,128)(2,1)}, bf16[512,1024]{1,0:T(8,128)(2,1)}, u32[]{:S(2)}, u32[]{:S(2)}) collective-permute-start(bf16[512,1024]{1,0:T(8,128)(2,1)} %get-tuple-element.1822), channel_id=1, source_target_pairs={{0,3},{1,0},{2,1},{3,2},{4,7},{5,4},{6,5},{7,6},{8,11},{9,8},{10,9... | collective-permute-start | bytes 3145736 | tf_op jit(solution)/shard_map/ppermute | solution.py:31
  20.9 1812.2 %reduce-scatter.9.cloned.1.call-start = ((), (), s32[]{:S(2)}) async-start(), calls=%async_computation.6 | async-start | bytes 5242880 | tf_op jit(solution)/shard_map/reduce_scatter | solution.py:181
  25.1 154.9 %copy-start.134 = (f32[2,2048]{1,0:T(2,128)S(1)}, f32[2,2048]{1,0:T(2,128)}, u32[]{:S(2)}) copy-start(f32[2,2048]{1,0:T(2,128)} %param.29) | copy-start | bytes 49156
  26.0 340.3 %copy-start.126 = (f32[1,1024]{1,0:T(1,128)}, f32[1,1024]{1,0:T(1,128)S(1)}, u32[]{:S(2)}) copy-start(f32[1,1024]{1,0:T(1,128)S(1)} %get-tuple-element.1840) | copy-start | bytes 12292
  27.8 338.4 %copy-start.136 = (f32[2,512]{1,0:T(2,128)}, f32[2,512]{1,0:T(2,128)S(1)}, u32[]{:S(2)}) copy-start(f32[2,512]{1,0:T(2,128)S(1)} %get-tuple-element.1842) | copy-start | bytes 12292
  29.8 240.6 %copy-start.141 = (f32[2,512]{1,0:T(2,128)}, f32[2,512]{1,0:T(2,128)S(1)}, u32[]{:S(2)}) copy-start(f32[2,512]{1,0:T(2,128)S(1)} %get-tuple-element.1855) | copy-start | bytes 12292
  156.3 90.9 %collective-permute-start.2 = (bf16[512,1024]{1,0:T(8,128)(2,1)}, bf16[512,1024]{1,0:T(8,128)(2,1)S(1)}, u32[]{:S(2)}, u32[]{:S(2)}) collective-permute-start(bf16[512,1024]{1,0:T(8,128)(2,1)} %collective-permute-done), channel_id=1, source_target_pairs={{0,1},{1,2},{2,3},{3,0},{4,5},{5,6},{6,7},{7,4},{8,9},{9,10},{10,1... | collective-permute-start | bytes 3145736 | tf_op jit(solution)/shard_map/ppermute | solution.py:26
  177.3 91.6 %collective-permute-start.5 = (bf16[512,1024]{1,0:T(8,128)(2,1)S(1)}, bf16[512,1024]{1,0:T(8,128)(2,1)S(1)}, u32[]{:S(2)}, u32[]{:S(2)}) collective-permute-start(bf16[512,1024]{1,0:T(8,128)(2,1)S(1)} %collective-permute-done.3), channel_id=1, source_target_pairs={{0,1},{1,2},{2,3},{3,0},{4,5},{5,6},{6,7},{7,4},{8,9},{9,10},{10,1... | collective-permute-start | bytes 3145736 | tf_op jit(solution)/shard_map/ppermute | solution.py:26
  386.5 196.1 %copy-start.137 = (f32[1,4,2,128]{3,1,2,0:T(4,128)S(1)}, f32[1,4,2,128]{3,1,2,0:T(4,128)}, u32[]{:S(2)}) copy-start(f32[1,4,2,128]{3,1,2,0:T(4,128)} %copy.386) | copy-start | bytes 12292
  642.7 76.8 %copy-start.45 = (f32[2,32,256]{2,1,0:T(8,128)}, f32[2,32,256]{2,1,0:T(8,128)S(1)}, u32[]{:S(2)}) copy-start(f32[2,32,256]{2,1,0:T(8,128)S(1)} %get-tuple-element.2371) | copy-start | bytes 196612 | tf_op jit(solution)/shard_map/transpose(jvp())/while
  663.0 56.5 %copy-start.49 = (pred[256,256]{1,0:T(8,128)(4,1)}, pred[256,256]{1,0:T(8,128)(4,1)S(1)}, u32[]{:S(2)}) copy-start(pred[256,256]{1,0:T(8,128)(4,1)S(1)} %iota_compare_fusion.5) | copy-start | bytes 196612 | tf_op jit(solution)/shard_map/transpose(jvp())/while
  859.4 76.8 %copy-start.45 = (f32[2,32,256]{2,1,0:T(8,128)}, f32[2,32,256]{2,1,0:T(8,128)S(1)}, u32[]{:S(2)}) copy-start(f32[2,32,256]{2,1,0:T(8,128)S(1)} %get-tuple-element.2371) | copy-start | bytes 196612 | tf_op jit(solution)/shard_map/transpose(jvp())/while
  879.6 56.5 %copy-start.49 = (pred[256,256]{1,0:T(8,128)(4,1)}, pred[256,256]{1,0:T(8,128)(4,1)S(1)}, u32[]{:S(2)}) copy-start(pred[256,256]{1,0:T(8,128)(4,1)S(1)} %iota_compare_fusion.5) | copy-start | bytes 196612 | tf_op jit(solution)/shard_map/transpose(jvp())/while
  1096.5 736.6 %reduce-scatter.11.cloned.1.call-start = ((), (), s32[]{:S(2)}) async-start(), calls=%async_computation.7 | async-start | bytes 5242880 | tf_op jit(solution)/shard_map/reduce_scatter | solution.py:181
  1099.1 210.9 %copy-start.142 = (f32[2,512]{1,0:T(2,128)S(1)}, f32[2,512]{1,0:T(2,128)}, u32[]{:S(2)}) copy-start(f32[2,512]{1,0:T(2,128)} %copy-done.141) | copy-start | bytes 12292
  1320.1 513.0 %reduce-scatter.7.cloned.1.call-start = ((), (), s32[]{:S(2)}) async-start(), calls=%async_computation.5 | async-start | bytes 11223040 | tf_op jit(solution)/shard_map/reduce_scatter | solution.py:178
  1337.3 652.4 %reduce-scatter.5.cloned.1.call-start = ((), (), s32[]{:S(2)}) async-start(), calls=%async_computation.4 | async-start | bytes 11223040 | tf_op jit(solution)/shard_map/reduce_scatter | solution.py:178
  1387.3 77.7 %copy-start.47 = (f32[2,32,256]{2,1,0:T(8,128)}, f32[2,32,256]{2,1,0:T(8,128)S(1)}, u32[]{:S(2)}) copy-start(f32[2,32,256]{2,1,0:T(8,128)S(1)} %get-tuple-element.2438) | copy-start | bytes 196612 | tf_op jit(solution)/shard_map/transpose(jvp())/while
  1407.8 57.2 %copy-start.51 = (pred[256,256]{1,0:T(8,128)(4,1)}, pred[256,256]{1,0:T(8,128)(4,1)S(1)}, u32[]{:S(2)}) copy-start(pred[256,256]{1,0:T(8,128)(4,1)S(1)} %iota_compare_fusion.6) | copy-start | bytes 196612 | tf_op jit(solution)/shard_map/transpose(jvp())/while
  1614.6 77.5 %copy-start.47 = (f32[2,32,256]{2,1,0:T(8,128)}, f32[2,32,256]{2,1,0:T(8,128)S(1)}, u32[]{:S(2)}) copy-start(f32[2,32,256]{2,1,0:T(8,128)S(1)} %get-tuple-element.2438) | copy-start | bytes 196612 | tf_op jit(solution)/shard_map/transpose(jvp())/while
  1634.9 57.2 %copy-start.51 = (pred[256,256]{1,0:T(8,128)(4,1)}, pred[256,256]{1,0:T(8,128)(4,1)S(1)}, u32[]{:S(2)}) copy-start(pred[256,256]{1,0:T(8,128)(4,1)S(1)} %iota_compare_fusion.6) | copy-start | bytes 196612 | tf_op jit(solution)/shard_map/transpose(jvp())/while
  1832.9 156.9 %copy-start.131 = (f32[1,4,2,128]{3,2,1,0:T(2,128)S(1)}, f32[1,4,2,128]{3,2,1,0:T(2,128)}, u32[]{:S(2)}) copy-start(f32[1,4,2,128]{3,2,1,0:T(2,128)} %get-tuple-element.1841) | copy-start | bytes 12292
  1833.0 271.0 %all-reduce.51.cloned.1.call-start = ((), (), s32[]{:S(2)}) async-start(), calls=%async_computation.13 | async-start | bytes 13172736 | tf_op jit(solution)/shard_map/psum | solution.py:186
  1989.8 241.4 %all-reduce.49.cloned.1.call-start = ((), (), s32[]{:S(2)}) async-start(), calls=%async_computation.8 | async-start | bytes 147456 | tf_op jit(solution)/shard_map/psum | solution.py:202
  2001.9 18.4 copy-start.143
  (255 other events, 1383.1 us)
Sparse Core Ops, SparseCore 0:
  11.2 153.1 all-gather.12
  166.5 199.6 all-gather.8
  367.8 158.6 all-gather.10
  527.9 79.2 all-gather.14
  1096.6 79.4 reduce-scatter.8
  1320.2 79.5 reduce-scatter.10
  1402.2 154.1 reduce-scatter.6
  1833.1 156.6 reduce-scatter.4
  1993.5 110.3 all-reduce.50
  2109.9 121.1 all-reduce.48
